TPU v7x, 32 devices: a whole 2x2x4 slice. The times are simulated.
32 devices in a mesh: shot: 2 (over y), gx: 4 (over z), sec: 2 (over x), gy: 2 (over core).
Axes of the slice: x: 2, y: 2, z: 4, core: 2. Of those that a mesh axis runs over, the one named last changes fastest.
Arguments:
- source_fields: float32 [8, 16, 32, 256], P('shot', 'sec', 'gx', 'gy'), parts along dimension 0, may hold values from -6 to 6
- receiver_fields: float32 [8, 16, 32, 256], P('shot', 'sec', 'gx', 'gy'), parts along dimension 0, may hold values from -6 to 6
- courant: float32 [16, 32, 256], P('sec', 'gx', 'gy'), may hold values from 0.05 to 0.15
- epsilon: float32 [16, 32, 256], P('sec', 'gx', 'gy'), may hold values from 0.05 to 0.3
- delta_param: float32 [16, 32, 256], P('sec', 'gx', 'gy'), may hold values from 0 to 0.15
- tilt_angle: float32 [16, 32, 256], P('sec', 'gx', 'gy'), may hold values from -0.8 to 0.8
- source_pos: int32 [6], P('shot'), parts along dimension 0, may hold values from 0 to 255, as said below
- wavelet: float32 [18], P('shot'), parts along dimension 0, may hold values from -24 to 24
- receiver_pos: int32 [512, 3], P('shot'), parts along dimension 0, may hold values from 0 to 255, as said below
- receiver_data: float32 [18, 256], P('shot'), parts along dimension 0, may hold values from -6 to 6
- step_counts: int32 [3], replicated, may hold values from 1 to 3, as said below
- offset_lags: int32 [48, 2], replicated, may hold values from -8 to 8, as said below
Outputs:
- offset_images: bfloat16 [96, 16, 32, 256], P('shot', 'sec', 'gx', 'gy'), parts along dimension 0
- source_out: float32 [8, 16, 32, 256], P('shot', 'sec', 'gx', 'gy'), parts along dimension 0
- receiver_out: float32 [8, 16, 32, 256], P('shot', 'sec', 'gx', 'gy'), parts along dimension 0
There are 2 independent parts, one for each index of `shot`. A program takes and returns all parts, laid end to end along the dimension named above; an argument that names none is the same for every part. Nothing has to cross between parts.
Inputs may be any that keep to these rules, and one draw needn't show every extreme that they name: `source_pos`: a grid cell: depth below 16, first horizontal below 32, second horizontal below 256; it lies on the last cell of the longest grid dimension and on cell 0 of another dimension. `receiver_pos`: grid cells: depth below 16, first horizontal below 32, second horizontal below 256; one receiver sits at the far corner of the grid and one at its anchor. `step_counts`: some snapshot takes all 3 steps. `offset_lags`: in each dimension some lag is 8 and some is minus 8.
All inputs are finite; a program needn't handle non-finite values.
Results may differ from a plain program's by a relative error of at most 0.001.
The roundings to bfloat16 on the way count: a program that leaves them out, or rounds other values in their place, can miss the bound.
Values may be sent and summed in bfloat16 or wider, within the bound.
No kernel may reach another device: no remote copies, remote signals or barrier semaphores. Data moves between devices by JAX's collectives and lax.ppermute only.
A program may use at most 64 MiB of HBM per device.

v0:
```python
import functools

import jax
import jax.numpy as jnp
from jax import lax
from jax.experimental import pallas as pl
from jax.experimental.pallas import tpu as pltpu
from jax.sharding import PartitionSpec as P


SNAPS = 3
STEPS = 3
LAG = 8
HALO = 4
ROWS = 4
WROWS = ROWS + 2 * HALO
ZB = 8
WZ = ZB + 2 * HALO
LANES = 128

F32 = jnp.float32
BF16 = jnp.bfloat16
VM = pl.BlockSpec(memory_space=pltpu.VMEM)
SM = pl.BlockSpec(memory_space=pltpu.SMEM)


def call(body, outs, n_smem, n_vmem, scratch=(), flops=100000, moved=1000000, mib=12):
    return pl.pallas_call(
        body,
        out_shape=outs,
        in_specs=[SM] * n_smem + [VM] * n_vmem,
        out_specs=[VM] * len(outs),
        scratch_shapes=list(scratch),
        cost_estimate=pl.CostEstimate(flops=flops, bytes_accessed=moved, transcendentals=0),
        compiler_params=pltpu.CompilerParams(vmem_limit_bytes=mib * 2**20),
    )


def half_swap(value):
    return pltpu.roll(value, HALO, 0)


def low_sublanes(shape):
    return lax.broadcasted_iota(jnp.int32, shape, 0) < HALO


def edges_of(first, second, sec_size):
    sub = low_sublanes(first.shape)
    top = jnp.where(sub, half_swap(first), second)
    bottom = jnp.where(sub, first, half_swap(second))
    if sec_size == 2:
        return [jnp.where(lax.axis_index("sec") == 0, top, bottom)]
    return [top, bottom]


def split_body(sec_size, src, rec, courant, epsilon, delta, tilt, keep, send, *edges):
    low = lax.axis_index("gy") == 0
    nz = len(edges) // 2

    def pair(j, picks, change=lambda v: v):
        for r in range(ROWS):
            mine, other = [], []
            for k, pick in enumerate(picks):
                lo = pick(pl.ds(r, ZB, stride=2 * ROWS))
                hi = pick(pl.ds(r + ROWS, ZB, stride=2 * ROWS))
                if k == 1:
                    lo, hi = change(lo), change(hi)
                mine.append(jnp.where(low, lo, hi))
                other.append(jnp.where(low, hi, lo))
                keep[2 * j + k, r] = mine[k]
                send[2 * j + k, r] = other[k]
            for ref, edge in zip(edges[:nz], edges_of(*mine, sec_size)):
                ref[j, r] = edge
            for ref, edge in zip(edges[nz:], edges_of(*other, sec_size)):
                ref[j, r] = edge

    for j in range(2):
        pair(j, [lambda s, m=2 * j + k: src[m, s, :] for k in range(2)])
        pair(2 + j, [lambda s, m=2 * j + k: rec[m, s, :] for k in range(2)])
    pair(4, [lambda s: courant[s, :], lambda s: epsilon[s, :]])
    pair(5, [lambda s: delta[s, :], lambda s: tilt[s, :]], jnp.sin)


def copy_body(source, target):
    target[...] = source[...]


def merge_body(keep, got, own):
    low = lax.axis_index("gy") == 0
    half = keep.shape[-1]

    def one(n, _):
        for r in range(ROWS):
            a, b = keep[n, r], got[n, r]
            own[n, r, :, :half] = jnp.where(low, a, b)
            own[n, r, :, half:] = jnp.where(low, b, a)
        return 0

    lax.fori_loop(0, own.shape[0], one, 0)


def inject_body(pos_t, data, out):
    x0 = lax.axis_index("gx") * (2 * ROWS) + lax.axis_index("gy") * ROWS - HALO
    z0 = lax.axis_index("sec") * ZB - HALO
    count, side = pos_t.shape[1], out.shape[3]
    slots = out.shape[0]
    zw = pos_t[0:1, :] - z0
    xw = pos_t[1:2, :] - x0
    inside = (zw >= 0) & (zw < WZ) & (xw >= 0) & (xw < WROWS)
    cell = jnp.where(inside, xw * WZ + zw, -1)
    hit = lax.broadcasted_iota(jnp.int32, (WROWS * WZ, count), 0) == cell
    columns = lax.broadcasted_iota(jnp.int32, (side, count), 0)
    onehot = jnp.where(columns == pos_t[2:3, :], 1.0, 0.0).astype(BF16)

    for t in range(slots):
        amount = data[t : t + 1, :]
        first = amount.astype(BF16).astype(F32)
        rest = amount - first
        second = rest.astype(BF16).astype(F32)
        third = rest - second
        total = None
        for part in (first, second, third):
            left = jnp.where(hit, part, 0.0).astype(BF16)
            term = lax.dot_general(
                left, onehot, (((1,), (1,)), ((), ())), preferred_element_type=F32
            )
            total = term if total is None else total + term
        out[t] = total.reshape(WROWS, WZ, side)


def assemble(dest, j, base, own, halos, here, padded=False):
    sec = lax.axis_index("sec")
    zero = jnp.zeros(own.shape[2:], F32)
    has_low = here & (sec > 0)
    has_high = here & (sec < lax.axis_size("sec") - 1)
    for r in range(ROWS):
        sub = low_sublanes(own.shape[2:])
        below = jnp.where(has_low, halos[0][j, r], zero)
        above = jnp.where(has_high, halos[-1][j, r], zero)
        lows = (below, half_swap(below))
        highs = (half_swap(above), above)
        for k in range(2):
            mid = half_swap(jnp.where(here, own[2 * j + k, r], zero))
            ref = dest(k)
            upper = jnp.where(sub, lows[k], mid)
            lower = jnp.where(sub, mid, highs[k])
            if padded:
                for h in range(own.shape[3] // LANES):
                    lanes = slice(h * LANES, (h + 1) * LANES)
                    ref[base + r, h, ZB : 2 * ZB, :] = upper[:, lanes]
                    ref[base + r, h, 2 * ZB : 3 * ZB, :] = lower[:, lanes]
            else:
                ref[base + r, 0:ZB, :] = upper
                ref[base + r, ZB:WZ, :] = lower


def round_body(number, sec_size, more, last, *refs):
    refs = list(refs)

    def take(n):
        out = refs[:n]
        del refs[:n]
        return out

    opening = number == 0
    nz = 1 if sec_size == 2 else 2
    counts, wavelet, source_pos = take(3)
    groups = [(take(1)[0], take(nz)) for _ in range(3)]
    if not opening:
        coef = take(1)[0]
    inject = take(1)[0]
    snaps_in = None if opening else take(1)[0]
    own_out, snaps = take(2)
    edge_outs = take(nz) if more else []
    final_send = take(1)[0] if last else None
    if opening:
        coef = take(1)[0]
    works = take(2)

    low = lax.axis_index("gy") == 0
    gx = lax.axis_index("gx")
    sec = lax.axis_index("sec")
    zero = jnp.int32(0)
    always = gx >= 0
    has_partner = jnp.where(low, gx, lax.axis_size("gx") - 1 - gx) > 0
    bases = [
        (jnp.int32(HALO), always),
        (jnp.where(low, HALO + ROWS, 0), always),
        (jnp.where(low, 0, HALO + ROWS), has_partner),
    ]

    def fields(i, _):
        for parity in range(2):
            for (base, here), (own, halos) in zip(bases, groups):
                put_at = lambda k, work=works[parity]: work.at[i, k]
                assemble(put_at, 2 * i + parity, base, own, halos, here, True)
        return 0

    lax.fori_loop(0, 2, fields, 0)

    if opening:
        for j in range(2):
            for (base, here), (own, halos) in zip(bases, groups):
                assemble(lambda k: coef.at[2 * j + k], 4 + j, base, own, halos, here)

        def derive(x, _):
            c = coef[0, x]
            s = coef[3, x]
            wx = s * s
            coef[1, x] = c * (1.0 + 2.0 * coef[1, x])
            coef[2, x] = c * (1.0 + 2.0 * coef[2, x])
            coef[3, x] = wx
            coef[4, x] = 0.5 * s * jnp.sqrt(1.0 - wx)
            return 0

        lax.fori_loop(1, WROWS - 1, derive, 0)
    else:
        snaps[...] = snaps_in[...]

    ends = []
    total = zero
    for s in range(SNAPS):
        total = total + counts[s]
        ends.append(total)
    first = number * HALO
    todo = jnp.clip(total - first, 0, HALO)
    n_lane = works[0].shape[3]
    side = n_lane * LANES
    n_depth = WZ // ZB
    v_sub = lax.broadcasted_iota(jnp.int32, (ZB, LANES), 0)
    v_lane = lax.broadcasted_iota(jnp.int32, (ZB, LANES), 1)
    keys = [(t, h) for t in range(n_depth) for h in range(n_lane)]
    x0 = gx * (2 * ROWS) + lax.axis_index("gy") * ROWS - HALO
    sx = source_pos[1] - x0
    sz = source_pos[0] - (sec * ZB - HALO)
    sy = source_pos[2]

    def own_cells(parity, section, which, r):
        start = ZB + HALO
        parts = [
            works[parity][section, which, HALO + r, h, start : start + ZB, :]
            for h in range(n_lane)
        ]
        return jnp.concatenate(parts, axis=1)

    def tiles(ref, *at):
        return {
            (t, h): ref[at + (slice(t * ZB, (t + 1) * ZB), slice(h * LANES, (h + 1) * LANES))]
            for t, h in keys
        }

    def cells(parity, section, which, x, shift=0):
        start = ZB + shift
        return {
            (t, h): works[parity][section, which, x, h, start + t * ZB : start + (t + 1) * ZB, :]
            for t, h in keys
        }

    def side_sum(v):
        left = {k: pltpu.roll(v[k], 1, 1) for k in keys}
        right = {k: pltpu.roll(v[k], LANES - 1, 1) for k in keys}
        out = {}
        for t, h in keys:
            a = jnp.where(v_lane == 0, left.get((t, h - 1), 0.0), left[t, h])
            b = jnp.where(v_lane == LANES - 1, right.get((t, h + 1), 0.0), right[t, h])
            out[t, h] = a + b
        return out

    def put(value, parity, section, which, x):
        for t, h in keys:
            works[parity][section, which, x, h, (t + 1) * ZB : (t + 2) * ZB, :] = value[t, h]

    def step(j):
        active = first + j
        slot = zero
        start = zero
        for s in range(SNAPS):
            slot = jnp.where(active >= start, s * STEPS + active - start, slot)
            start = ends[s]
        cur = j % 2
        new = 1 - cur
        margin = todo - 1 - j

        def one_row(x, c, ce, cd, wx, wm, section):
            p, pm, pp = (cells(cur, section, 0, x + d) for d in (0, -1, 1))
            q, qm, qp = (cells(cur, section, 1, x + d) for d in (0, -1, 1))
            pu, pmu, ppu = (cells(cur, section, 0, x + d, 1) for d in (0, -1, 1))
            pd, pmd, ppd = (cells(cur, section, 0, x + d, -1) for d in (0, -1, 1))
            qu, qmu, qpu = (cells(cur, section, 1, x + d, 1) for d in (0, -1, 1))
            qd, qmd, qpd = (cells(cur, section, 1, x + d, -1) for d in (0, -1, 1))
            ys = side_sum(p)
            po = cells(new, section, 0, x)
            qo = cells(new, section, 1, x)
            extra = tiles(inject, slot, x) if section == 1 else None
            new_p, new_q = {}, {}
            for k in keys:
                zz = pu[k] + pd[k]
                xx = pp[k] + pm[k]
                xz = (ppu[k] - pmu[k]) - (ppd[k] - pmd[k])
                horiz = (xx + ys[k] - 4.0 * p[k]) + wx[k] * (zz - xx) - wm[k] * xz
                q2 = 2.0 * q[k]
                qz = qu[k] + qd[k]
                qx = qp[k] + qm[k]
                qxz = (qpu[k] - qmu[k]) - (qpd[k] - qmd[k])
                vert = c[k] * ((qz - q2) + wx[k] * (qx - qz) + wm[k] * qxz)
                new_p[k] = (2.0 * p[k] - po[k]) + (ce[k] * horiz + vert)
                new_q[k] = (q2 - qo[k]) + (cd[k] * horiz + vert)
                if extra is not None:
                    new_p[k] = new_p[k] + extra[k]
                    new_q[k] = new_q[k] + extra[k]
            put(new_p, new, section, 0, x)
            put(new_q, new, section, 1, x)

        def rows(i, _):
            for u in range(2):
                x = HALO - margin + 2 * i + u
                weights = [tiles(coef, n, x) for n in range(5)]
                for section in range(2):
                    one_row(x, *weights, section)
            return 0

        lax.fori_loop(0, ROWS // 2 + margin, rows, 0)

        @pl.when((sx >= 0) & (sx < WROWS))
        def _():
            amount = wavelet[slot]
            for t, h in keys:
                hit = (v_sub == sz - t * ZB) & (v_lane == sy - h * LANES)
                here = jnp.where(hit, amount, 0.0)
                for which in range(2):
                    at = (0, which, sx, h, slice((t + 1) * ZB, (t + 2) * ZB))
                    works[new][at] = works[new][at] + here

        for s in range(SNAPS):

            @pl.when(active + 1 == ends[s])
            def _():
                for r in range(ROWS):
                    both = [own_cells(new, section, 0, r) for section in range(2)]
                    snaps[s, r] = jnp.concatenate(both, axis=0).astype(BF16)

    for j in range(HALO):
        pl.when(j < todo)(functools.partial(step, j))

    odd = todo % 2 == 1
    for section in range(2):
        for old in range(2):
            for r in range(ROWS):
                both = []
                for which in range(2):
                    value = jnp.where(
                        odd,
                        own_cells(1 - old, section, which, r),
                        own_cells(old, section, which, r),
                    )
                    member = section * 4 + old * 2 + which
                    own_out[member, r] = value
                    if last:
                        final_send[member, r] = jnp.where(
                            low, value[:, side // 2 :], value[:, : side // 2]
                        )
                    both.append(value)
                if more:
                    for ref, edge in zip(edge_outs, edges_of(both[0], both[1], sec_size)):
                        ref[section * 2 + old, r] = edge


def fields_body(own, got, src, rec):
    low = lax.axis_index("gy") == 0
    half = got.shape[-1]
    mine = jnp.where(low, 0, ROWS)
    other = jnp.where(low, ROWS, 0)
    for member in range(8):
        dest = src if member < 4 else rec
        base = (member % 4) * ZB * 2 * ROWS
        for r in range(ROWS):
            value = own[member, r]
            value = jnp.where(low, value[:, :half], value[:, half:])
            dest[pl.ds(base + mine + r, ZB, stride=2 * ROWS), :] = value
            dest[pl.ds(base + other + r, ZB, stride=2 * ROWS), :] = got[member, r]


def image_body(lags, snaps, sib, near, far, sib_near, sib_far, images, rows, table, flip):
    core = lax.axis_index("gy")
    gx = lax.axis_index("gx")
    low = core == 0
    half = images.shape[3]
    side = rows.shape[-1]
    span = 6 * ROWS
    mine_on = jnp.where(low, gx, lax.axis_size("gx") - 1 - gx) > 0
    sib_on = jnp.where(low, lax.axis_size("gx") - 1 - gx, gx) > 0
    pieces = (
        (near, jnp.where(low, ROWS, 4 * ROWS), mine_on),
        (far, jnp.where(low, 0, 5 * ROWS), mine_on),
        (snaps, jnp.where(low, 2 * ROWS, 3 * ROWS), None),
        (sib, jnp.where(low, 3 * ROWS, 2 * ROWS), None),
        (sib_near, jnp.where(low, 4 * ROWS, ROWS), sib_on),
        (sib_far, jnp.where(low, 5 * ROWS, 0), sib_on),
    )
    for piece, base, here in pieces:
        for s in range(SNAPS):
            for r in range(ROWS):
                value = piece[s, r]
                if here is not None:
                    value = jnp.where(here, value, jnp.zeros_like(value))
                rows[s * span + base + r] = value

    cells = rows[...].reshape(SNAPS * span * 2 * ZB, side)
    lane = lax.broadcasted_iota(jnp.int32, (side, 2 * half), 1)
    second = (lane >= half).astype(jnp.int32)
    gap = lax.broadcasted_iota(jnp.int32, (side, 2 * half), 0) - core * half - lane + second * (half + 1)

    def shifts(i, _):
        for u in range(3):
            m = 3 * i + u
            pick = jnp.where(gap == LAG - 2 * m, 1.0, 0.0).astype(BF16)
            moved = jnp.dot(cells, pick, preferred_element_type=F32)
            for h in range(2):
                part = moved[:, h * half : (h + 1) * half]
                table[2 * m + h] = part.reshape(SNAPS * span, 2 * ZB, half)
        return 0

    lax.fori_loop(0, (LAG + 1) // 3, shifts, 0)

    count = lags.shape[1]
    group = next(g for g in (4, 3, 2, 1) if count % g == 0)

    def some_lags(i, _):
        for u in range(group):
            l = i * group + u
            lx = lags[0, l]
            ly = lags[1, l]
            total = None
            for s in range(SNAPS):
                at = s * span + 2 * ROWS
                a = table[LAG + ly, pl.ds(at - lx, 2 * ROWS), 0:ZB, :]
                b = table[LAG - ly, pl.ds(at + lx, 2 * ROWS), ZB : 2 * ZB, :]
                total = a * b if total is None else total + a * b
            for x in range(2 * ROWS):
                flip[u, pl.ds(x, ZB, stride=2 * ROWS), :] = total[x]
            images[l] = flip[u].reshape(ZB, 2 * ROWS, half).astype(BF16)
        return 0

    lax.fori_loop(0, count // group, some_lags, 0)


def local(
    source_fields,
    receiver_fields,
    courant,
    epsilon,
    delta_param,
    tilt_angle,
    source_pos,
    wavelet,
    receiver_pos,
    receiver_data,
    step_counts,
    offset_lags,
):
    sec_size = lax.axis_size("sec")
    gx_size = lax.axis_size("gx")
    depth_cells, wide_cells, half = courant.shape
    side = 2 * half
    shots, nz = lax.axis_size("shot"), (1 if sec_size == 2 else 2)
    axes = ("shot", "gx", "sec", "gy")

    def permute(x, move):
        def rank(d):
            return ((d[0] * gx_size + d[1]) * sec_size + d[2]) * 2 + d[3]

        pairs = [
            (rank((n, g, s, c)), rank(move(n, g, s, c)))
            for n in range(shots)
            for g in range(gx_size)
            for s in range(sec_size)
            for c in range(2)
        ]
        return lax.ppermute(x, axes, pairs)

    def sibling(x):
        return permute(x, lambda n, g, s, c: (n, g, s, 1 - c))

    def facing(n, g, s, c):
        other = g - 1 if c == 0 else g + 1
        if 0 <= other < gx_size:
            return (n, other, s, 1 - c)
        return ((n + 1) % shots, g, s, c)

    def abreast(n, g, s, c):
        other = g + 1 if c == 0 else g - 1
        if 0 <= other < gx_size:
            return (n, other, s, c)
        return (n, g, s, 1 - c)

    def partner(x):
        return permute(x, facing)

    def depth_halos(edges, flip=0):
        ups = [permute(edges[0], lambda n, g, s, c: (n, g, (s + 1) % sec_size, c ^ flip))]
        if nz == 2:
            ups.append(permute(edges[1], lambda n, g, s, c: (n, g, (s - 1) % sec_size, c ^ flip)))
        return ups

    def flat(x):
        return x.reshape(x.shape[:-3] + (depth_cells * wide_cells, half))

    part = jax.ShapeDtypeStruct((12, ROWS, ZB, half), F32)
    edge_part = jax.ShapeDtypeStruct((6, ROWS, ZB, half), F32)
    edge8 = jax.ShapeDtypeStruct((4, ROWS, ZB, side), F32)
    keep, send, *edges = call(
        functools.partial(split_body, sec_size), [part, part] + [edge_part] * (2 * nz), 0, 6, mib=60
    )(
        flat(source_fields),
        flat(receiver_fields),
        flat(courant),
        flat(epsilon),
        flat(delta_param),
        flat(tilt_angle),
    )

    def merge(a, b):
        out = jax.ShapeDtypeStruct(a.shape[:-1] + (side,), F32)
        return call(merge_body, [out], 0, 2)(a, b)[0]

    near_edges = depth_halos(edges[:nz])
    far_edges = depth_halos(edges[nz:], 1)
    par_keep = partner(keep)
    par_send = permute(send, abreast)
    got = sibling(send)
    sib_keep = sibling(keep)
    (keep,) = call(copy_body, [part], 0, 1)(keep)
    (send,) = call(copy_body, [part], 0, 1)(send)
    owns = [merge(keep, got), merge(send, sib_keep), merge(par_send, par_keep)]

    slots = receiver_data.shape[0]
    (inject,) = call(
        inject_body, [jax.ShapeDtypeStruct((slots, WROWS, WZ, side), F32)], 0, 2
    )(receiver_pos.T, receiver_data)

    def share(owns, halos):
        sib_halos = [sibling(h) for h in halos]
        par_halos = [partner(h) for h in halos]
        return list(zip(owns, (halos, sib_halos, par_halos)))

    def exchange(own, edges):
        return share([own, sibling(own), partner(own)], depth_halos(edges))

    snap_type = jax.ShapeDtypeStruct((SNAPS, ROWS, 2 * ZB, side), BF16)
    own_type = jax.ShapeDtypeStruct((8, ROWS, ZB, side), F32)
    fin_type = jax.ShapeDtypeStruct((8, ROWS, ZB, half), F32)

    coef_type = jax.ShapeDtypeStruct((5, WROWS, WZ, side), F32)

    def run_round(number, groups, coef, snaps, more, last):
        args = [step_counts, wavelet, source_pos]
        for own_, halos in groups:
            args += [own_] + list(halos)
        if number:
            args.append(coef)
        args.append(inject)
        if number:
            args.append(snaps)
        outs = [own_type, snap_type]
        if more:
            outs += [edge8] * nz
        if last:
            outs += [fin_type]
        if not number:
            outs += [coef_type]
        return call(
            functools.partial(round_body, number, sec_size, more, last),
            outs,
            3,
            len(args) - 3,
            [pltpu.VMEM((2, 2, WROWS, side // LANES, 2 * ZB + WZ, LANES), F32)] * 2,
            10000000,
            3000000,
            16,
        )(*args)

    halos = [merge(a, b) for a, b in zip(near_edges, far_edges)]
    groups = share(owns, halos)
    own, snaps, *rest = run_round(0, groups, None, None, True, False)
    edges, coef = rest[:nz], rest[nz]
    own, snaps, *rest = run_round(1, exchange(own, edges), coef, snaps, True, True)
    edges, final_send = rest[:nz], rest[nz]

    def third(own, snaps, final_send, *edges):
        return tuple(run_round(2, exchange(own, list(edges)), coef, snaps, False, True))

    def done(own, snaps, final_send, *edges):
        return own, snaps, final_send

    own, snaps, final_send = lax.cond(
        jnp.sum(step_counts) > 2 * HALO, third, done, own, snaps, final_send, *edges
    )
    final_got = sibling(final_send)
    sib = sibling(snaps)
    near, far = partner(snaps), partner(sib)
    sib_near, sib_far = sibling(near), sibling(far)
    n_lags = offset_lags.shape[0]
    out = jax.ShapeDtypeStruct((4 * depth_cells * wide_cells, half), F32)
    src, rec = call(fields_body, [out, out], 0, 2)(own, final_got)
    (images,) = call(
        image_body,
        [jax.ShapeDtypeStruct((n_lags, depth_cells, wide_cells, half), BF16)],
        1,
        6,
        [
            pltpu.VMEM((SNAPS * 6 * ROWS, 2 * ZB, side), BF16),
            pltpu.VMEM((2 * LAG + 2, SNAPS * 6 * ROWS, 2 * ZB, half), F32),
            pltpu.VMEM((4, ZB * 2 * ROWS, half), F32),
        ],
        10000000,
        3000000,
        24,
    )(offset_lags.T, snaps, sib, near, far, sib_near, sib_far)
    shape = (4, depth_cells, wide_cells, half)
    return images, src.reshape(shape), rec.reshape(shape)


def solution(mesh):
    placed = (
        P("shot", "sec", "gx", "gy"),
        P("shot", "sec", "gx", "gy"),
        P("sec", "gx", "gy"),
        P("sec", "gx", "gy"),
        P("sec", "gx", "gy"),
        P("sec", "gx", "gy"),
        P("shot"),
        P("shot"),
        P("shot", None),
        P("shot", None),
        P(),
        P(),
    )
    return jax.shard_map(
        local,
        mesh=mesh,
        in_specs=placed,
        out_specs=(
            P("shot", "sec", "gx", "gy"),
            P("shot", "sec", "gx", "gy"),
            P("shot", "sec", "gx", "gy"),
        ),
        check_vma=False,
    )
```

profile of v0, /device:TPU:0, one launch (start us, length us, event | category | flops | bytes accessed | tf_op | source)
XLA Modules:
  0.0 48.1 jit_solution(9507274594550220717)
XLA Ops:
  0.6 2.0 %shard_map.139 = (f32[12,4,8,128]{3,2,1,0:T(8,128)}, f32[12,4,8,128]{3,2,1,0:T(8,128)}, f32[6,4,8,128]{3,2,1,0:T(8,128)}, f32[6,4,8,128]{3,2,1,0:T(8,128)}) custom-call(f32[4,64,128]{2,1,0:T(8,128)} %bitcast.12, f32[4,64,128]{2,1,0:T(8,128)} %bitcast.13, f32[64,128]{1,0:T(8,128)} %bitcast.14, f32[64,128]{1,0:T(8,128)} %bitcast.15, f32[64,128]{1,0:T(8,128)} %bitcast.16, ...), custom_call_target="tpu_custom_call" | custom-call | flops 100000 | bytes 1000000 | tf_op jit(solution)/shard_map/pallas_call | solution.py:511
  3.1 2.5 %collective-permute-start.6 = (f32[6,4,8,128]{3,2,1,0:T(8,128)}, f32[6,4,8,128]{3,2,1,0:T(8,128)S(1)}, u32[]{:S(2)}, u32[]{:S(2)}) collective-permute-start(f32[6,4,8,128]{3,2,1,0:T(8,128)} %get-tuple-element.52), channel_id=1, source_target_pairs={{0,2},{1,3},{2,0},{3,1},{4,6},{5,7},{6,4},{7,5},{8,10},{9,11},{10,... | collective-permute-start | bytes 294920 | tf_op jit(solution)/shard_map/ppermute | solution.py:479
  5.7 1.8 %collective-permute-start.11 = (f32[12,4,8,128]{3,2,1,0:T(8,128)}, f32[12,4,8,128]{3,2,1,0:T(8,128)S(1)}, u32[]{:S(2)}, u32[]{:S(2)}) collective-permute-start(f32[12,4,8,128]{3,2,1,0:T(8,128)} %get-tuple-element.50.source), channel_id=1, source_target_pairs={{0,16},{1,4},{2,18},{3,6},{4,1},{5,8},{6,3},{7,10},{8,5},{9,12},{1... | collective-permute-start | bytes 589832 | tf_op jit(solution)/shard_map/ppermute | solution.py:479
  7.6 2.0 %collective-permute-done.6.keep = f32[6,4,8,128]{3,2,1,0:T(8,128)S(1)} collective-permute-done((f32[6,4,8,128]{3,2,1,0:T(8,128)}, f32[6,4,8,128]{3,2,1,0:T(8,128)S(1)}, u32[]{:S(2)}, u32[]{:S(2)}) %collective-permute-start.6) | collective-permute-done | bytes 98336 | tf_op jit(solution)/shard_map/ppermute | solution.py:479
  9.5 1.6 %collective-permute-done.7.got = f32[6,4,8,128]{3,2,1,0:T(8,128)S(1)} collective-permute-done((f32[6,4,8,128]{3,2,1,0:T(8,128)}, f32[6,4,8,128]{3,2,1,0:T(8,128)S(1)}, u32[]{:S(2)}, u32[]{:S(2)}) %collective-permute-start.7) | collective-permute-done | bytes 98336 | tf_op jit(solution)/shard_map/ppermute | solution.py:479
  11.2 1.6 %collective-permute-start.12 = (f32[6,4,8,256]{3,2,1,0:T(8,128)S(1)}, f32[6,4,8,256]{3,2,1,0:T(8,128)S(1)}, u32[]{:S(2)}, u32[]{:S(2)}) collective-permute-start(f32[6,4,8,256]{3,2,1,0:T(8,128)S(1)} %shard_map.142.refs_4_), channel_id=1, source_target_pairs={{0,16},{1,4},{2,18},{3,6},{4,1},{5,8},{6,3},{7,10},{8,5},{9,12},{1... | collective-permute-start | bytes 589832 | tf_op jit(solution)/shard_map/ppermute | solution.py:479
  12.9 0.9 %copy-done.1 = f32[12,4,8,128]{3,2,1,0:T(8,128)S(1)} copy-done((f32[12,4,8,128]{3,2,1,0:T(8,128)S(1)}, f32[12,4,8,128]{3,2,1,0:T(8,128)}, u32[]{:S(2)}) %copy-start.1) | copy-done | bytes 196632
  13.9 0.9 %copy-done = f32[12,4,8,128]{3,2,1,0:T(8,128)S(1)} copy-done((f32[12,4,8,128]{3,2,1,0:T(8,128)S(1)}, f32[12,4,8,128]{3,2,1,0:T(8,128)}, u32[]{:S(2)}) %copy-start) | copy-done | bytes 196632
  14.8 0.7 %copy-done.2 = f32[9,256]{1,0:T(8,128)S(1)} copy-done((f32[9,256]{1,0:T(8,128)S(1)}, f32[9,256]{1,0:T(8,128)}, u32[]{:S(2)}) %copy-start.2) | copy-done | bytes 9240
  15.6 0.7 %copy-done.3 = s32[256,3]{0,1:T(4,128)S(1)} copy-done((s32[256,3]{0,1:T(4,128)S(1)}, s32[256,3]{0,1:T(4,128)}, u32[]{:S(2)}) %copy-start.3) | copy-done | bytes 3096
  16.2 1.3 %shard_map.146.refs_9_.refs_10_ = f32[9,12,16,256]{3,2,1,0:T(8,128)S(1)} custom-call(s32[3,256]{1,0:T(4,128)S(1)} %bitcast.10, f32[9,256]{1,0:T(8,128)S(1)} %copy-done.2), custom_call_target="tpu_custom_call" | custom-call | flops 100000 | bytes 1000000 | tf_op jit(solution)/shard_map/pallas_call | solution.py:537
  17.9 4.1 %shard_map.147 = (f32[8,4,8,256]{3,2,1,0:T(8,128)S(1)}, bf16[3,4,16,256]{3,2,1,0:T(8,128)(2,1)S(1)}, f32[4,4,8,256]{3,2,1,0:T(8,128)S(1)}, f32[5,12,16,256]{3,2,1,0:T(8,128)}) custom-call(s32[3]{0:T(128)S(1)} %copy-done.5, f32[9]{0:T(128)S(1)} %copy-done.6, s32[3]{0:T(128)S(1)} %copy-done.7, f32[12,4,8,256]{3,2,1,0:T(8,128)S(1)} %shard_map.141.refs_3_, ...), custom_call_target="tpu_custom_call" | custom-call | flops 10000000 | bytes 3000000 | tf_op jit(solution)/shard_map/pallas_call | solution.py:571
  22.1 1.5 %collective-permute-start.13 = (f32[4,4,8,256]{3,2,1,0:T(8,128)S(1)}, f32[4,4,8,256]{3,2,1,0:T(8,128)S(1)}, u32[]{:S(2)}, u32[]{:S(2)}) collective-permute-start(f32[4,4,8,256]{3,2,1,0:T(8,128)S(1)} %get-tuple-element.55), channel_id=1, source_target_pairs={{0,2},{1,3},{2,0},{3,1},{4,6},{5,7},{6,4},{7,5},{8,10},{9,11},{10,... | collective-permute-start | bytes 393224 | tf_op jit(solution)/shard_map/ppermute | solution.py:479
  23.6 1.5 %collective-permute-start.16 = (f32[8,4,8,256]{3,2,1,0:T(8,128)S(1)}, f32[8,4,8,256]{3,2,1,0:T(8,128)S(1)}, u32[]{:S(2)}, u32[]{:S(2)}) collective-permute-start(f32[8,4,8,256]{3,2,1,0:T(8,128)S(1)} %get-tuple-element.54.refs_3_), channel_id=1, source_target_pairs={{0,16},{1,4},{2,18},{3,6},{4,1},{5,8},{6,3},{7,10},{8,5},{9,12},{1... | collective-permute-start | bytes 786440 | tf_op jit(solution)/shard_map/ppermute | solution.py:479
  25.3 2.6 %collective-permute-done.13.refs_4_ = f32[4,4,8,256]{3,2,1,0:T(8,128)S(1)} collective-permute-done((f32[4,4,8,256]{3,2,1,0:T(8,128)S(1)}, f32[4,4,8,256]{3,2,1,0:T(8,128)S(1)}, u32[]{:S(2)}, u32[]{:S(2)}) %collective-permute-start.13) | collective-permute-done | bytes 131104 | tf_op jit(solution)/shard_map/ppermute | solution.py:479
  27.8 1.2 %collective-permute-start.17 = (f32[4,4,8,256]{3,2,1,0:T(8,128)S(1)}, f32[4,4,8,256]{3,2,1,0:T(8,128)S(1)}, u32[]{:S(2)}, u32[]{:S(2)}) collective-permute-start(f32[4,4,8,256]{3,2,1,0:T(8,128)S(1)} %collective-permute-done.13.refs_4_), channel_id=1, source_target_pairs={{0,16},{1,4},{2,18},{3,6},{4,1},{5,8},{6,3},{7,10},{8,5},{9,12},{1... | collective-permute-start | bytes 393224 | tf_op jit(solution)/shard_map/ppermute | solution.py:479
  30.5 2.3 %collective-permute-done.17.refs_8_ = f32[4,4,8,256]{3,2,1,0:T(8,128)S(1)} collective-permute-done((f32[4,4,8,256]{3,2,1,0:T(8,128)S(1)}, f32[4,4,8,256]{3,2,1,0:T(8,128)S(1)}, u32[]{:S(2)}, u32[]{:S(2)}) %collective-permute-start.17) | collective-permute-done | bytes 131104 | tf_op jit(solution)/shard_map/ppermute | solution.py:479
  32.8 3.7 %shard_map.148 = (f32[8,4,8,256]{3,2,1,0:T(8,128)S(1)}, bf16[3,4,16,256]{3,2,1,0:T(8,128)(2,1)S(1)}, f32[4,4,8,256]{3,2,1,0:T(8,128)S(1)}, f32[8,4,8,128]{3,2,1,0:T(8,128)S(1)}) custom-call(s32[3]{0:T(128)S(1)} %copy-done.5, f32[9]{0:T(128)S(1)} %copy-done.6, s32[3]{0:T(128)S(1)} %copy-done.7, f32[8,4,8,256]{3,2,1,0:T(8,128)S(1)} %get-tuple-element.54.refs_3_, ...), custom_call_target="tpu_custom_call" | custom-call | flops 10000000 | bytes 3000000 | tf_op jit(solution)/shard_map/pallas_call | solution.py:571
  36.6 1.3 %collective-permute-start.19 = (bf16[3,4,16,256]{3,2,1,0:T(8,128)(2,1)S(1)}, bf16[3,4,16,256]{3,2,1,0:T(8,128)(2,1)S(1)}, u32[]{:S(2)}, u32[]{:S(2)}) collective-permute-start(bf16[3,4,16,256]{3,2,1,0:T(8,128)(2,1)S(1)} %get-tuple-element.62.snaps), channel_id=1, source_target_pairs={{0,16},{1,4},{2,18},{3,6},{4,1},{5,8},{6,3},{7,10},{8,5},{9,12},{1... | collective-permute-start | bytes 294920 | tf_op jit(solution)/shard_map/ppermute | solution.py:479
  37.9 1.2 %collective-permute-start.20 = (bf16[3,4,16,256]{3,2,1,0:T(8,128)(2,1)S(1)}, bf16[3,4,16,256]{3,2,1,0:T(8,128)(2,1)S(1)}, u32[]{:S(2)}, u32[]{:S(2)}) collective-permute-start(bf16[3,4,16,256]{3,2,1,0:T(8,128)(2,1)S(1)} %collective-permute-done.18.sib), channel_id=1, source_target_pairs={{0,16},{1,4},{2,18},{3,6},{4,1},{5,8},{6,3},{7,10},{8,5},{9,12},{1... | collective-permute-start | bytes 294920 | tf_op jit(solution)/shard_map/ppermute | solution.py:479
  39.1 2.2 %collective-permute-done.19.near = bf16[3,4,16,256]{3,2,1,0:T(8,128)(2,1)S(1)} collective-permute-done((bf16[3,4,16,256]{3,2,1,0:T(8,128)(2,1)S(1)}, bf16[3,4,16,256]{3,2,1,0:T(8,128)(2,1)S(1)}, u32[]{:S(2)}, u32[]{:S(2)}) %collective-permute-start.19) | collective-permute-done | bytes 98336 | tf_op jit(solution)/shard_map/ppermute | solution.py:479
  41.4 1.1 %collective-permute-done.20.far = bf16[3,4,16,256]{3,2,1,0:T(8,128)(2,1)S(1)} collective-permute-done((bf16[3,4,16,256]{3,2,1,0:T(8,128)(2,1)S(1)}, bf16[3,4,16,256]{3,2,1,0:T(8,128)(2,1)S(1)}, u32[]{:S(2)}, u32[]{:S(2)}) %collective-permute-start.20) | collective-permute-done | bytes 98336 | tf_op jit(solution)/shard_map/ppermute | solution.py:479
  42.5 0.8 %shard_map.150 = (f32[256,128]{1,0:T(8,128)}, f32[256,128]{1,0:T(8,128)}) custom-call(f32[8,4,8,256]{3,2,1,0:T(8,128)S(1)} %get-tuple-element.63.own, f32[8,4,8,128]{3,2,1,0:T(8,128)S(1)} %collective-permute-done.23.got), custom_call_target="tpu_custom_call" | custom-call | flops 100000 | bytes 1000000 | tf_op jit(solution)/shard_map/pallas_call | solution.py:604
  43.8 4.3 %shard_map.149 = bf16[48,8,8,128]{3,2,1,0:T(8,128)(2,1)} custom-call(s32[2,48]{1,0:T(2,128)S(1)} %bitcast.11, bf16[3,4,16,256]{3,2,1,0:T(8,128)(2,1)S(1)} %get-tuple-element.62.snaps, bf16[3,4,16,256]{3,2,1,0:T(8,128)(2,1)S(1)} %collective-permute-done.18.sib, bf16[3,4,16,256]{3,2,1,0:T(8,128)(2,1)S(1)} %collective-permute-done.19.near, ...), custom_call_target="tpu_custom_call" | custom-call | flops 10000000 | bytes 3000000 | tf_op jit(solution)/shard_map/pallas_call | solution.py:605
  (44 shorter events, 2.9 us)
Async XLA Ops:
  2.6 10.1 %collective-permute-start.8 = (f32[12,4,8,128]{3,2,1,0:T(8,128)}, f32[12,4,8,128]{3,2,1,0:T(8,128)S(1)}, u32[]{:S(2)}, u32[]{:S(2)}) collective-permute-start(f32[12,4,8,128]{3,2,1,0:T(8,128)} %get-tuple-element.50.source), channel_id=1, source_target_pairs={{0,1},{1,0},{2,3},{3,2},{4,5},{5,4},{6,7},{7,6},{8,9},{9,8},{10,11... | collective-permute-start | bytes 589832 | tf_op jit(solution)/shard_map/ppermute | solution.py:479
  3.1 6.4 %collective-permute-start.6 = (f32[6,4,8,128]{3,2,1,0:T(8,128)}, f32[6,4,8,128]{3,2,1,0:T(8,128)S(1)}, u32[]{:S(2)}, u32[]{:S(2)}) collective-permute-start(f32[6,4,8,128]{3,2,1,0:T(8,128)} %get-tuple-element.52), channel_id=1, source_target_pairs={{0,2},{1,3},{2,0},{3,1},{4,6},{5,7},{6,4},{7,5},{8,10},{9,11},{10,... | collective-permute-start | bytes 294920 | tf_op jit(solution)/shard_map/ppermute | solution.py:479
  5.7 5.5 %collective-permute-start.7 = (f32[6,4,8,128]{3,2,1,0:T(8,128)}, f32[6,4,8,128]{3,2,1,0:T(8,128)S(1)}, u32[]{:S(2)}, u32[]{:S(2)}) collective-permute-start(f32[6,4,8,128]{3,2,1,0:T(8,128)} %get-tuple-element.53), channel_id=1, source_target_pairs={{0,3},{1,2},{2,1},{3,0},{4,7},{5,6},{6,5},{7,4},{8,11},{9,10},{10,... | collective-permute-start | bytes 294920 | tf_op jit(solution)/shard_map/ppermute | solution.py:479
  5.7 11.9 %collective-permute-start.11 = (f32[12,4,8,128]{3,2,1,0:T(8,128)}, f32[12,4,8,128]{3,2,1,0:T(8,128)S(1)}, u32[]{:S(2)}, u32[]{:S(2)}) collective-permute-start(f32[12,4,8,128]{3,2,1,0:T(8,128)} %get-tuple-element.50.source), channel_id=1, source_target_pairs={{0,16},{1,4},{2,18},{3,6},{4,1},{5,8},{6,3},{7,10},{8,5},{9,12},{1... | collective-permute-start | bytes 589832 | tf_op jit(solution)/shard_map/ppermute | solution.py:479
  7.5 10.2 %collective-permute-start.10 = (f32[12,4,8,128]{3,2,1,0:T(8,128)}, f32[12,4,8,128]{3,2,1,0:T(8,128)S(1)}, u32[]{:S(2)}, u32[]{:S(2)}) collective-permute-start(f32[12,4,8,128]{3,2,1,0:T(8,128)} %get-tuple-element.51.source), channel_id=1, source_target_pairs={{0,4},{1,0},{2,6},{3,2},{4,8},{5,1},{6,10},{7,3},{8,12},{9,5},{10,... | collective-permute-start | bytes 589832 | tf_op jit(solution)/shard_map/ppermute | solution.py:479
  9.5 8.3 %collective-permute-start.5 = (f32[12,4,8,128]{3,2,1,0:T(8,128)}, f32[12,4,8,128]{3,2,1,0:T(8,128)S(1)}, u32[]{:S(2)}, u32[]{:S(2)}) collective-permute-start(f32[12,4,8,128]{3,2,1,0:T(8,128)} %get-tuple-element.51.source), channel_id=1, source_target_pairs={{0,1},{1,0},{2,3},{3,2},{4,5},{5,4},{6,7},{7,6},{8,9},{9,8},{10,11... | collective-permute-start | bytes 589832 | tf_op jit(solution)/shard_map/ppermute | solution.py:479
  11.2 6.7 %collective-permute-start.12 = (f32[6,4,8,256]{3,2,1,0:T(8,128)S(1)}, f32[6,4,8,256]{3,2,1,0:T(8,128)S(1)}, u32[]{:S(2)}, u32[]{:S(2)}) collective-permute-start(f32[6,4,8,256]{3,2,1,0:T(8,128)S(1)} %shard_map.142.refs_4_), channel_id=1, source_target_pairs={{0,16},{1,4},{2,18},{3,6},{4,1},{5,8},{6,3},{7,10},{8,5},{9,12},{1... | collective-permute-start | bytes 589832 | tf_op jit(solution)/shard_map/ppermute | solution.py:479
  12.8 5.1 %collective-permute-start.9 = (f32[6,4,8,256]{3,2,1,0:T(8,128)S(1)}, f32[6,4,8,256]{3,2,1,0:T(8,128)S(1)}, u32[]{:S(2)}, u32[]{:S(2)}) collective-permute-start(f32[6,4,8,256]{3,2,1,0:T(8,128)S(1)} %shard_map.142.refs_4_), channel_id=1, source_target_pairs={{0,1},{1,0},{2,3},{3,2},{4,5},{5,4},{6,7},{7,6},{8,9},{9,8},{10,11... | collective-permute-start | bytes 589832 | tf_op jit(solution)/shard_map/ppermute | solution.py:479
  13.9 0.9 %copy-start = (f32[12,4,8,128]{3,2,1,0:T(8,128)S(1)}, f32[12,4,8,128]{3,2,1,0:T(8,128)}, u32[]{:S(2)}) copy-start(f32[12,4,8,128]{3,2,1,0:T(8,128)} %get-tuple-element.51.source) | copy-start | bytes 589828
  16.2 1.7 %copy-start.5 = (s32[3]{0:T(128)S(1)}, s32[3]{0:T(128)}, u32[]{:S(2)}) copy-start(s32[3]{0:T(128)} %refs_0_.3) | copy-start | bytes 40
  16.2 1.7 %copy-start.6 = (f32[9]{0:T(128)S(1)}, f32[9]{0:T(128)}, u32[]{:S(2)}) copy-start(f32[9]{0:T(128)} %refs_1_.3) | copy-start | bytes 112
  16.2 1.7 %copy-start.7 = (s32[3]{0:T(128)S(1)}, s32[3]{0:T(128)}, u32[]{:S(2)}) copy-start(s32[3]{0:T(128)} %refs_2_.3) | copy-start | bytes 40
  22.1 5.7 %collective-permute-start.13 = (f32[4,4,8,256]{3,2,1,0:T(8,128)S(1)}, f32[4,4,8,256]{3,2,1,0:T(8,128)S(1)}, u32[]{:S(2)}, u32[]{:S(2)}) collective-permute-start(f32[4,4,8,256]{3,2,1,0:T(8,128)S(1)} %get-tuple-element.55), channel_id=1, source_target_pairs={{0,2},{1,3},{2,0},{3,1},{4,6},{5,7},{6,4},{7,5},{8,10},{9,11},{10,... | collective-permute-start | bytes 393224 | tf_op jit(solution)/shard_map/ppermute | solution.py:479
  23.6 9.2 %collective-permute-start.16 = (f32[8,4,8,256]{3,2,1,0:T(8,128)S(1)}, f32[8,4,8,256]{3,2,1,0:T(8,128)S(1)}, u32[]{:S(2)}, u32[]{:S(2)}) collective-permute-start(f32[8,4,8,256]{3,2,1,0:T(8,128)S(1)} %get-tuple-element.54.refs_3_), channel_id=1, source_target_pairs={{0,16},{1,4},{2,18},{3,6},{4,1},{5,8},{6,3},{7,10},{8,5},{9,12},{1... | collective-permute-start | bytes 786440 | tf_op jit(solution)/shard_map/ppermute | solution.py:479
  25.1 7.7 %collective-permute-start.14 = (f32[8,4,8,256]{3,2,1,0:T(8,128)S(1)}, f32[8,4,8,256]{3,2,1,0:T(8,128)S(1)}, u32[]{:S(2)}, u32[]{:S(2)}) collective-permute-start(f32[8,4,8,256]{3,2,1,0:T(8,128)S(1)} %get-tuple-element.54.refs_3_), channel_id=1, source_target_pairs={{0,1},{1,0},{2,3},{3,2},{4,5},{5,4},{6,7},{7,6},{8,9},{9,8},{10,11... | collective-permute-start | bytes 786440 | tf_op jit(solution)/shard_map/ppermute | solution.py:479
  27.8 5.0 %collective-permute-start.17 = (f32[4,4,8,256]{3,2,1,0:T(8,128)S(1)}, f32[4,4,8,256]{3,2,1,0:T(8,128)S(1)}, u32[]{:S(2)}, u32[]{:S(2)}) collective-permute-start(f32[4,4,8,256]{3,2,1,0:T(8,128)S(1)} %collective-permute-done.13.refs_4_), channel_id=1, source_target_pairs={{0,16},{1,4},{2,18},{3,6},{4,1},{5,8},{6,3},{7,10},{8,5},{9,12},{1... | collective-permute-start | bytes 393224 | tf_op jit(solution)/shard_map/ppermute | solution.py:479
  29.0 3.8 %collective-permute-start.15 = (f32[4,4,8,256]{3,2,1,0:T(8,128)S(1)}, f32[4,4,8,256]{3,2,1,0:T(8,128)S(1)}, u32[]{:S(2)}, u32[]{:S(2)}) collective-permute-start(f32[4,4,8,256]{3,2,1,0:T(8,128)S(1)} %collective-permute-done.13.refs_4_), channel_id=1, source_target_pairs={{0,1},{1,0},{2,3},{3,2},{4,5},{5,4},{6,7},{7,6},{8,9},{9,8},{10,11... | collective-permute-start | bytes 393224 | tf_op jit(solution)/shard_map/ppermute | solution.py:479
  36.5 7.3 %copy-start.4 = (s32[48,2]{0,1:T(2,128)S(1)}, s32[48,2]{0,1:T(2,128)}, u32[]{:S(2)}) copy-start(s32[48,2]{0,1:T(2,128)} %param.25) | copy-start | bytes 1156
  36.5 1.4 %collective-permute-start.18 = (bf16[3,4,16,256]{3,2,1,0:T(8,128)(2,1)S(1)}, bf16[3,4,16,256]{3,2,1,0:T(8,128)(2,1)S(1)}, u32[]{:S(2)}, u32[]{:S(2)}) collective-permute-start(bf16[3,4,16,256]{3,2,1,0:T(8,128)(2,1)S(1)} %get-tuple-element.62.snaps), channel_id=1, source_target_pairs={{0,1},{1,0},{2,3},{3,2},{4,5},{5,4},{6,7},{7,6},{8,9},{9,8},{10,11... | collective-permute-start | bytes 294920 | tf_op jit(solution)/shard_map/ppermute | solution.py:479
  36.6 4.7 %collective-permute-start.19 = (bf16[3,4,16,256]{3,2,1,0:T(8,128)(2,1)S(1)}, bf16[3,4,16,256]{3,2,1,0:T(8,128)(2,1)S(1)}, u32[]{:S(2)}, u32[]{:S(2)}) collective-permute-start(bf16[3,4,16,256]{3,2,1,0:T(8,128)(2,1)S(1)} %get-tuple-element.62.snaps), channel_id=1, source_target_pairs={{0,16},{1,4},{2,18},{3,6},{4,1},{5,8},{6,3},{7,10},{8,5},{9,12},{1... | collective-permute-start | bytes 294920 | tf_op jit(solution)/shard_map/ppermute | solution.py:479
  37.9 4.6 %collective-permute-start.20 = (bf16[3,4,16,256]{3,2,1,0:T(8,128)(2,1)S(1)}, bf16[3,4,16,256]{3,2,1,0:T(8,128)(2,1)S(1)}, u32[]{:S(2)}, u32[]{:S(2)}) collective-permute-start(bf16[3,4,16,256]{3,2,1,0:T(8,128)(2,1)S(1)} %collective-permute-done.18.sib), channel_id=1, source_target_pairs={{0,16},{1,4},{2,18},{3,6},{4,1},{5,8},{6,3},{7,10},{8,5},{9,12},{1... | collective-permute-start | bytes 294920 | tf_op jit(solution)/shard_map/ppermute | solution.py:479
  39.1 3.4 %collective-permute-start.23 = (f32[8,4,8,128]{3,2,1,0:T(8,128)S(1)}, f32[8,4,8,128]{3,2,1,0:T(8,128)S(1)}, u32[]{:S(2)}, u32[]{:S(2)}) collective-permute-start(f32[8,4,8,128]{3,2,1,0:T(8,128)S(1)} %get-tuple-element.64), channel_id=1, source_target_pairs={{0,1},{1,0},{2,3},{3,2},{4,5},{5,4},{6,7},{7,6},{8,9},{9,8},{10,11... | collective-permute-start | bytes 393224 | tf_op jit(solution)/shard_map/ppermute | solution.py:479
  41.3 2.0 %collective-permute-start.21 = (bf16[3,4,16,256]{3,2,1,0:T(8,128)(2,1)S(1)}, bf16[3,4,16,256]{3,2,1,0:T(8,128)(2,1)S(1)}, u32[]{:S(2)}, u32[]{:S(2)}) collective-permute-start(bf16[3,4,16,256]{3,2,1,0:T(8,128)(2,1)S(1)} %collective-permute-done.19.near), channel_id=1, source_target_pairs={{0,1},{1,0},{2,3},{3,2},{4,5},{5,4},{6,7},{7,6},{8,9},{9,8},{10,11... | collective-permute-start | bytes 294920 | tf_op jit(solution)/shard_map/ppermute | solution.py:479
  42.5 1.3 %collective-permute-start.22 = (bf16[3,4,16,256]{3,2,1,0:T(8,128)(2,1)S(1)}, bf16[3,4,16,256]{3,2,1,0:T(8,128)(2,1)S(1)}, u32[]{:S(2)}, u32[]{:S(2)}) collective-permute-start(bf16[3,4,16,256]{3,2,1,0:T(8,128)(2,1)S(1)} %collective-permute-done.20.far), channel_id=1, source_target_pairs={{0,1},{1,0},{2,3},{3,2},{4,5},{5,4},{6,7},{7,6},{8,9},{9,8},{10,11... | collective-permute-start | bytes 294920 | tf_op jit(solution)/shard_map/ppermute | solution.py:479
  (3 other events, 2.3 us)
where the time goes:
time: 48.4 us; the launch traced here: 48.1 us
  Pallas kernels  16.5 us (34%)
  starting transfers between devices  13.9 us (29%)
  waiting for transfers between devices  12.3 us (25%)
  local copies, waits for them, and re-layouts  3.26 us (7%)
  between operations  1.46 us (3%)
  other arithmetic  0.63 us (1%)
    ppermute x19, starting transfers between devices, permute(): return lax.ppermute(x, axes, pairs)  13.9 us
    ppermute x19, waiting for transfers between devices, permute(): return lax.ppermute(x, axes, pairs)  12.3 us
    pallas_call x2, Pallas kernels, run_round(): call(functools.partial(round_body, number, sec_size, more, last), outs, 3...  7.8 us
    pallas_call x1, Pallas kernels, local(): call(image_body, [jax.ShapeDtypeStruct((n_lags, depth_cells, wide_cells,...  4.32 us
    unnamed x16, local copies, waits for them, and re-layouts  3.26 us
    pallas_call x1, Pallas kernels, local(): call(functools.partial(split_body, sec_size), [part, part] + [edge_part]...  2.01 us
    pallas_call x1, Pallas kernels, local(): call(inject_body, [jax.ShapeDtypeStruct((slots, WROWS, WZ, side), F32)],...  1.31 us
  transfers between devices with their start and end apart: 19, of which 7 were waited for; matrix products, arithmetic and copies ran while one was open for 1% of the time, Pallas kernels for 5%

commit v1 on v0

--- a/solution.py
+++ b/solution.py
@@ -404,6 +404,8 @@
                 if here is not None:
                     value = jnp.where(here, value, jnp.zeros_like(value))
                 rows[s * span + base + r] = value
+                middle = value.astype(F32)
+                table[LAG, s * span + base + r] = jnp.where(low, middle[:, :half], middle[:, half:])
 
     cells = rows[...].reshape(SNAPS * span * 2 * ZB, side)
     lane = lax.broadcasted_iota(jnp.int32, (side, 2 * half), 1)
@@ -411,16 +413,17 @@
     gap = lax.broadcasted_iota(jnp.int32, (side, 2 * half), 0) - core * half - lane + second * (half + 1)
 
     def shifts(i, _):
-        for u in range(3):
-            m = 3 * i + u
-            pick = jnp.where(gap == LAG - 2 * m, 1.0, 0.0).astype(BF16)
-            moved = jnp.dot(cells, pick, preferred_element_type=F32)
-            for h in range(2):
-                part = moved[:, h * half : (h + 1) * half]
-                table[2 * m + h] = part.reshape(SNAPS * span, 2 * ZB, half)
+        for first in (0, LAG + 1):
+            for u in range(2):
+                at = first + 4 * i + 2 * u
+                pick = jnp.where(gap == LAG - at, 1.0, 0.0).astype(BF16)
+                moved = jnp.dot(cells, pick, preferred_element_type=F32)
+                for h in range(2):
+                    part = moved[:, h * half : (h + 1) * half]
+                    table[at + h] = part.reshape(SNAPS * span, 2 * ZB, half)
         return 0
 
-    lax.fori_loop(0, (LAG + 1) // 3, shifts, 0)
+    lax.fori_loop(0, LAG // 4, shifts, 0)
 
     count = lags.shape[1]
     group = next(g for g in (4, 3, 2, 1) if count % g == 0)
@@ -609,7 +612,7 @@
         6,
         [
             pltpu.VMEM((SNAPS * 6 * ROWS, 2 * ZB, side), BF16),
-            pltpu.VMEM((2 * LAG + 2, SNAPS * 6 * ROWS, 2 * ZB, half), F32),
+            pltpu.VMEM((2 * LAG + 1, SNAPS * 6 * ROWS, 2 * ZB, half), F32),
             pltpu.VMEM((4, ZB * 2 * ROWS, half), F32),
         ],
         10000000,

time: 48.4 us -> 48.2 us (level)
  no operation moved by 1% of the time
where the time goes in v1:
time: 48.2 us; the launch traced here: 47.8 us
  Pallas kernels  16.3 us (34%)
  starting transfers between devices  13.9 us (29%)
  waiting for transfers between devices  12.3 us (26%)
  local copies, waits for them, and re-layouts  3.26 us (7%)
  between operations  1.46 us (3%)
  other arithmetic  0.63 us (1%)
    ppermute x19, starting transfers between devices, permute(): return lax.ppermute(x, axes, pairs)  13.9 us
    ppermute x19, waiting for transfers between devices, permute(): return lax.ppermute(x, axes, pairs)  12.3 us
    pallas_call x2, Pallas kernels, run_round(): call(functools.partial(round_body, number, sec_size, more, last), outs, 3...  7.8 us
    pallas_call x1, Pallas kernels, local(): call(image_body, [jax.ShapeDtypeStruct((n_lags, depth_cells, wide_cells,...  4.05 us
    unnamed x16, local copies, waits for them, and re-layouts  3.26 us
    pallas_call x1, Pallas kernels, local(): call(functools.partial(split_body, sec_size), [part, part] + [edge_part]...  2.01 us
    pallas_call x1, Pallas kernels, local(): call(inject_body, [jax.ShapeDtypeStruct((slots, WROWS, WZ, side), F32)],...  1.31 us
  transfers between devices with their start and end apart: 19, of which 7 were waited for; matrix products, arithmetic and copies ran while one was open for 1% of the time, Pallas kernels for 5%

profile of v1, /device:TPU:0, one launch (start us, length us, event | category | flops | bytes accessed | tf_op | source)
XLA Modules:
  0.0 47.8 jit_solution(6158895941935479226)
XLA Ops:
  0.6 2.0 %shard_map.139 = (f32[12,4,8,128]{3,2,1,0:T(8,128)}, f32[12,4,8,128]{3,2,1,0:T(8,128)}, f32[6,4,8,128]{3,2,1,0:T(8,128)}, f32[6,4,8,128]{3,2,1,0:T(8,128)}) custom-call(f32[4,64,128]{2,1,0:T(8,128)} %bitcast.12, f32[4,64,128]{2,1,0:T(8,128)} %bitcast.13, f32[64,128]{1,0:T(8,128)} %bitcast.14, f32[64,128]{1,0:T(8,128)} %bitcast.15, f32[64,128]{1,0:T(8,128)} %bitcast.16, ...), custom_call_target="tpu_custom_call" | custom-call | flops 100000 | bytes 1000000 | tf_op jit(solution)/shard_map/pallas_call | solution.py:514
  3.1 2.5 %collective-permute-start.6 = (f32[6,4,8,128]{3,2,1,0:T(8,128)}, f32[6,4,8,128]{3,2,1,0:T(8,128)S(1)}, u32[]{:S(2)}, u32[]{:S(2)}) collective-permute-start(f32[6,4,8,128]{3,2,1,0:T(8,128)} %get-tuple-element.52), channel_id=1, source_target_pairs={{0,2},{1,3},{2,0},{3,1},{4,6},{5,7},{6,4},{7,5},{8,10},{9,11},{10,... | collective-permute-start | bytes 294920 | tf_op jit(solution)/shard_map/ppermute | solution.py:482
  5.7 1.8 %collective-permute-start.11 = (f32[12,4,8,128]{3,2,1,0:T(8,128)}, f32[12,4,8,128]{3,2,1,0:T(8,128)S(1)}, u32[]{:S(2)}, u32[]{:S(2)}) collective-permute-start(f32[12,4,8,128]{3,2,1,0:T(8,128)} %get-tuple-element.50.source), channel_id=1, source_target_pairs={{0,16},{1,4},{2,18},{3,6},{4,1},{5,8},{6,3},{7,10},{8,5},{9,12},{1... | collective-permute-start | bytes 589832 | tf_op jit(solution)/shard_map/ppermute | solution.py:482
  7.6 2.0 %collective-permute-done.6.keep = f32[6,4,8,128]{3,2,1,0:T(8,128)S(1)} collective-permute-done((f32[6,4,8,128]{3,2,1,0:T(8,128)}, f32[6,4,8,128]{3,2,1,0:T(8,128)S(1)}, u32[]{:S(2)}, u32[]{:S(2)}) %collective-permute-start.6) | collective-permute-done | bytes 98336 | tf_op jit(solution)/shard_map/ppermute | solution.py:482
  9.5 1.6 %collective-permute-done.7.got = f32[6,4,8,128]{3,2,1,0:T(8,128)S(1)} collective-permute-done((f32[6,4,8,128]{3,2,1,0:T(8,128)}, f32[6,4,8,128]{3,2,1,0:T(8,128)S(1)}, u32[]{:S(2)}, u32[]{:S(2)}) %collective-permute-start.7) | collective-permute-done | bytes 98336 | tf_op jit(solution)/shard_map/ppermute | solution.py:482
  11.2 1.6 %collective-permute-start.12 = (f32[6,4,8,256]{3,2,1,0:T(8,128)S(1)}, f32[6,4,8,256]{3,2,1,0:T(8,128)S(1)}, u32[]{:S(2)}, u32[]{:S(2)}) collective-permute-start(f32[6,4,8,256]{3,2,1,0:T(8,128)S(1)} %shard_map.142.refs_4_), channel_id=1, source_target_pairs={{0,16},{1,4},{2,18},{3,6},{4,1},{5,8},{6,3},{7,10},{8,5},{9,12},{1... | collective-permute-start | bytes 589832 | tf_op jit(solution)/shard_map/ppermute | solution.py:482
  12.9 0.9 %copy-done.1 = f32[12,4,8,128]{3,2,1,0:T(8,128)S(1)} copy-done((f32[12,4,8,128]{3,2,1,0:T(8,128)S(1)}, f32[12,4,8,128]{3,2,1,0:T(8,128)}, u32[]{:S(2)}) %copy-start.1) | copy-done | bytes 196632
  13.9 0.9 %copy-done = f32[12,4,8,128]{3,2,1,0:T(8,128)S(1)} copy-done((f32[12,4,8,128]{3,2,1,0:T(8,128)S(1)}, f32[12,4,8,128]{3,2,1,0:T(8,128)}, u32[]{:S(2)}) %copy-start) | copy-done | bytes 196632
  14.8 0.7 %copy-done.2 = f32[9,256]{1,0:T(8,128)S(1)} copy-done((f32[9,256]{1,0:T(8,128)S(1)}, f32[9,256]{1,0:T(8,128)}, u32[]{:S(2)}) %copy-start.2) | copy-done | bytes 9240
  15.6 0.7 %copy-done.3 = s32[256,3]{0,1:T(4,128)S(1)} copy-done((s32[256,3]{0,1:T(4,128)S(1)}, s32[256,3]{0,1:T(4,128)}, u32[]{:S(2)}) %copy-start.3) | copy-done | bytes 3096
  16.2 1.3 %shard_map.146.refs_9_.refs_10_ = f32[9,12,16,256]{3,2,1,0:T(8,128)S(1)} custom-call(s32[3,256]{1,0:T(4,128)S(1)} %bitcast.10, f32[9,256]{1,0:T(8,128)S(1)} %copy-done.2), custom_call_target="tpu_custom_call" | custom-call | flops 100000 | bytes 1000000 | tf_op jit(solution)/shard_map/pallas_call | solution.py:540
  17.9 4.1 %shard_map.147 = (f32[8,4,8,256]{3,2,1,0:T(8,128)S(1)}, bf16[3,4,16,256]{3,2,1,0:T(8,128)(2,1)S(1)}, f32[4,4,8,256]{3,2,1,0:T(8,128)S(1)}, f32[5,12,16,256]{3,2,1,0:T(8,128)}) custom-call(s32[3]{0:T(128)S(1)} %copy-done.5, f32[9]{0:T(128)S(1)} %copy-done.6, s32[3]{0:T(128)S(1)} %copy-done.7, f32[12,4,8,256]{3,2,1,0:T(8,128)S(1)} %shard_map.141.refs_3_, ...), custom_call_target="tpu_custom_call" | custom-call | flops 10000000 | bytes 3000000 | tf_op jit(solution)/shard_map/pallas_call | solution.py:574
  22.1 1.5 %collective-permute-start.13 = (f32[4,4,8,256]{3,2,1,0:T(8,128)S(1)}, f32[4,4,8,256]{3,2,1,0:T(8,128)S(1)}, u32[]{:S(2)}, u32[]{:S(2)}) collective-permute-start(f32[4,4,8,256]{3,2,1,0:T(8,128)S(1)} %get-tuple-element.55), channel_id=1, source_target_pairs={{0,2},{1,3},{2,0},{3,1},{4,6},{5,7},{6,4},{7,5},{8,10},{9,11},{10,... | collective-permute-start | bytes 393224 | tf_op jit(solution)/shard_map/ppermute | solution.py:482
  23.6 1.5 %collective-permute-start.16 = (f32[8,4,8,256]{3,2,1,0:T(8,128)S(1)}, f32[8,4,8,256]{3,2,1,0:T(8,128)S(1)}, u32[]{:S(2)}, u32[]{:S(2)}) collective-permute-start(f32[8,4,8,256]{3,2,1,0:T(8,128)S(1)} %get-tuple-element.54.refs_3_), channel_id=1, source_target_pairs={{0,16},{1,4},{2,18},{3,6},{4,1},{5,8},{6,3},{7,10},{8,5},{9,12},{1... | collective-permute-start | bytes 786440 | tf_op jit(solution)/shard_map/ppermute | solution.py:482
  25.3 2.6 %collective-permute-done.13.refs_4_ = f32[4,4,8,256]{3,2,1,0:T(8,128)S(1)} collective-permute-done((f32[4,4,8,256]{3,2,1,0:T(8,128)S(1)}, f32[4,4,8,256]{3,2,1,0:T(8,128)S(1)}, u32[]{:S(2)}, u32[]{:S(2)}) %collective-permute-start.13) | collective-permute-done | bytes 131104 | tf_op jit(solution)/shard_map/ppermute | solution.py:482
  27.8 1.2 %collective-permute-start.17 = (f32[4,4,8,256]{3,2,1,0:T(8,128)S(1)}, f32[4,4,8,256]{3,2,1,0:T(8,128)S(1)}, u32[]{:S(2)}, u32[]{:S(2)}) collective-permute-start(f32[4,4,8,256]{3,2,1,0:T(8,128)S(1)} %collective-permute-done.13.refs_4_), channel_id=1, source_target_pairs={{0,16},{1,4},{2,18},{3,6},{4,1},{5,8},{6,3},{7,10},{8,5},{9,12},{1... | collective-permute-start | bytes 393224 | tf_op jit(solution)/shard_map/ppermute | solution.py:482
  30.5 2.3 %collective-permute-done.17.refs_8_ = f32[4,4,8,256]{3,2,1,0:T(8,128)S(1)} collective-permute-done((f32[4,4,8,256]{3,2,1,0:T(8,128)S(1)}, f32[4,4,8,256]{3,2,1,0:T(8,128)S(1)}, u32[]{:S(2)}, u32[]{:S(2)}) %collective-permute-start.17) | collective-permute-done | bytes 131104 | tf_op jit(solution)/shard_map/ppermute | solution.py:482
  32.8 3.7 %shard_map.148 = (f32[8,4,8,256]{3,2,1,0:T(8,128)S(1)}, bf16[3,4,16,256]{3,2,1,0:T(8,128)(2,1)S(1)}, f32[4,4,8,256]{3,2,1,0:T(8,128)S(1)}, f32[8,4,8,128]{3,2,1,0:T(8,128)S(1)}) custom-call(s32[3]{0:T(128)S(1)} %copy-done.5, f32[9]{0:T(128)S(1)} %copy-done.6, s32[3]{0:T(128)S(1)} %copy-done.7, f32[8,4,8,256]{3,2,1,0:T(8,128)S(1)} %get-tuple-element.54.refs_3_, ...), custom_call_target="tpu_custom_call" | custom-call | flops 10000000 | bytes 3000000 | tf_op jit(solution)/shard_map/pallas_call | solution.py:574
  36.6 1.3 %collective-permute-start.19 = (bf16[3,4,16,256]{3,2,1,0:T(8,128)(2,1)S(1)}, bf16[3,4,16,256]{3,2,1,0:T(8,128)(2,1)S(1)}, u32[]{:S(2)}, u32[]{:S(2)}) collective-permute-start(bf16[3,4,16,256]{3,2,1,0:T(8,128)(2,1)S(1)} %get-tuple-element.62.snaps), channel_id=1, source_target_pairs={{0,16},{1,4},{2,18},{3,6},{4,1},{5,8},{6,3},{7,10},{8,5},{9,12},{1... | collective-permute-start | bytes 294920 | tf_op jit(solution)/shard_map/ppermute | solution.py:482
  37.9 1.2 %collective-permute-start.20 = (bf16[3,4,16,256]{3,2,1,0:T(8,128)(2,1)S(1)}, bf16[3,4,16,256]{3,2,1,0:T(8,128)(2,1)S(1)}, u32[]{:S(2)}, u32[]{:S(2)}) collective-permute-start(bf16[3,4,16,256]{3,2,1,0:T(8,128)(2,1)S(1)} %collective-permute-done.18.sib), channel_id=1, source_target_pairs={{0,16},{1,4},{2,18},{3,6},{4,1},{5,8},{6,3},{7,10},{8,5},{9,12},{1... | collective-permute-start | bytes 294920 | tf_op jit(solution)/shard_map/ppermute | solution.py:482
  39.1 2.2 %collective-permute-done.19.near = bf16[3,4,16,256]{3,2,1,0:T(8,128)(2,1)S(1)} collective-permute-done((bf16[3,4,16,256]{3,2,1,0:T(8,128)(2,1)S(1)}, bf16[3,4,16,256]{3,2,1,0:T(8,128)(2,1)S(1)}, u32[]{:S(2)}, u32[]{:S(2)}) %collective-permute-start.19) | collective-permute-done | bytes 98336 | tf_op jit(solution)/shard_map/ppermute | solution.py:482
  41.4 1.1 %collective-permute-done.20.far = bf16[3,4,16,256]{3,2,1,0:T(8,128)(2,1)S(1)} collective-permute-done((bf16[3,4,16,256]{3,2,1,0:T(8,128)(2,1)S(1)}, bf16[3,4,16,256]{3,2,1,0:T(8,128)(2,1)S(1)}, u32[]{:S(2)}, u32[]{:S(2)}) %collective-permute-start.20) | collective-permute-done | bytes 98336 | tf_op jit(solution)/shard_map/ppermute | solution.py:482
  42.5 0.8 %shard_map.150 = (f32[256,128]{1,0:T(8,128)}, f32[256,128]{1,0:T(8,128)}) custom-call(f32[8,4,8,256]{3,2,1,0:T(8,128)S(1)} %get-tuple-element.63.own, f32[8,4,8,128]{3,2,1,0:T(8,128)S(1)} %collective-permute-done.23.got), custom_call_target="tpu_custom_call" | custom-call | flops 100000 | bytes 1000000 | tf_op jit(solution)/shard_map/pallas_call | solution.py:607
  43.8 4.1 %shard_map.149 = bf16[48,8,8,128]{3,2,1,0:T(8,128)(2,1)} custom-call(s32[2,48]{1,0:T(2,128)S(1)} %bitcast.11, bf16[3,4,16,256]{3,2,1,0:T(8,128)(2,1)S(1)} %get-tuple-element.62.snaps, bf16[3,4,16,256]{3,2,1,0:T(8,128)(2,1)S(1)} %collective-permute-done.18.sib, bf16[3,4,16,256]{3,2,1,0:T(8,128)(2,1)S(1)} %collective-permute-done.19.near, ...), custom_call_target="tpu_custom_call" | custom-call | flops 10000000 | bytes 3000000 | tf_op jit(solution)/shard_map/pallas_call | solution.py:608
  (44 shorter events, 2.9 us)
Async XLA Ops:
  2.6 10.1 %collective-permute-start.8 = (f32[12,4,8,128]{3,2,1,0:T(8,128)}, f32[12,4,8,128]{3,2,1,0:T(8,128)S(1)}, u32[]{:S(2)}, u32[]{:S(2)}) collective-permute-start(f32[12,4,8,128]{3,2,1,0:T(8,128)} %get-tuple-element.50.source), channel_id=1, source_target_pairs={{0,1},{1,0},{2,3},{3,2},{4,5},{5,4},{6,7},{7,6},{8,9},{9,8},{10,11... | collective-permute-start | bytes 589832 | tf_op jit(solution)/shard_map/ppermute | solution.py:482
  3.1 6.4 %collective-permute-start.6 = (f32[6,4,8,128]{3,2,1,0:T(8,128)}, f32[6,4,8,128]{3,2,1,0:T(8,128)S(1)}, u32[]{:S(2)}, u32[]{:S(2)}) collective-permute-start(f32[6,4,8,128]{3,2,1,0:T(8,128)} %get-tuple-element.52), channel_id=1, source_target_pairs={{0,2},{1,3},{2,0},{3,1},{4,6},{5,7},{6,4},{7,5},{8,10},{9,11},{10,... | collective-permute-start | bytes 294920 | tf_op jit(solution)/shard_map/ppermute | solution.py:482
  5.7 5.5 %collective-permute-start.7 = (f32[6,4,8,128]{3,2,1,0:T(8,128)}, f32[6,4,8,128]{3,2,1,0:T(8,128)S(1)}, u32[]{:S(2)}, u32[]{:S(2)}) collective-permute-start(f32[6,4,8,128]{3,2,1,0:T(8,128)} %get-tuple-element.53), channel_id=1, source_target_pairs={{0,3},{1,2},{2,1},{3,0},{4,7},{5,6},{6,5},{7,4},{8,11},{9,10},{10,... | collective-permute-start | bytes 294920 | tf_op jit(solution)/shard_map/ppermute | solution.py:482
  5.7 11.9 %collective-permute-start.11 = (f32[12,4,8,128]{3,2,1,0:T(8,128)}, f32[12,4,8,128]{3,2,1,0:T(8,128)S(1)}, u32[]{:S(2)}, u32[]{:S(2)}) collective-permute-start(f32[12,4,8,128]{3,2,1,0:T(8,128)} %get-tuple-element.50.source), channel_id=1, source_target_pairs={{0,16},{1,4},{2,18},{3,6},{4,1},{5,8},{6,3},{7,10},{8,5},{9,12},{1... | collective-permute-start | bytes 589832 | tf_op jit(solution)/shard_map/ppermute | solution.py:482
  7.5 10.2 %collective-permute-start.10 = (f32[12,4,8,128]{3,2,1,0:T(8,128)}, f32[12,4,8,128]{3,2,1,0:T(8,128)S(1)}, u32[]{:S(2)}, u32[]{:S(2)}) collective-permute-start(f32[12,4,8,128]{3,2,1,0:T(8,128)} %get-tuple-element.51.source), channel_id=1, source_target_pairs={{0,4},{1,0},{2,6},{3,2},{4,8},{5,1},{6,10},{7,3},{8,12},{9,5},{10,... | collective-permute-start | bytes 589832 | tf_op jit(solution)/shard_map/ppermute | solution.py:482
  9.5 8.3 %collective-permute-start.5 = (f32[12,4,8,128]{3,2,1,0:T(8,128)}, f32[12,4,8,128]{3,2,1,0:T(8,128)S(1)}, u32[]{:S(2)}, u32[]{:S(2)}) collective-permute-start(f32[12,4,8,128]{3,2,1,0:T(8,128)} %get-tuple-element.51.source), channel_id=1, source_target_pairs={{0,1},{1,0},{2,3},{3,2},{4,5},{5,4},{6,7},{7,6},{8,9},{9,8},{10,11... | collective-permute-start | bytes 589832 | tf_op jit(solution)/shard_map/ppermute | solution.py:482
  11.2 6.7 %collective-permute-start.12 = (f32[6,4,8,256]{3,2,1,0:T(8,128)S(1)}, f32[6,4,8,256]{3,2,1,0:T(8,128)S(1)}, u32[]{:S(2)}, u32[]{:S(2)}) collective-permute-start(f32[6,4,8,256]{3,2,1,0:T(8,128)S(1)} %shard_map.142.refs_4_), channel_id=1, source_target_pairs={{0,16},{1,4},{2,18},{3,6},{4,1},{5,8},{6,3},{7,10},{8,5},{9,12},{1... | collective-permute-start | bytes 589832 | tf_op jit(solution)/shard_map/ppermute | solution.py:482
  12.8 5.1 %collective-permute-start.9 = (f32[6,4,8,256]{3,2,1,0:T(8,128)S(1)}, f32[6,4,8,256]{3,2,1,0:T(8,128)S(1)}, u32[]{:S(2)}, u32[]{:S(2)}) collective-permute-start(f32[6,4,8,256]{3,2,1,0:T(8,128)S(1)} %shard_map.142.refs_4_), channel_id=1, source_target_pairs={{0,1},{1,0},{2,3},{3,2},{4,5},{5,4},{6,7},{7,6},{8,9},{9,8},{10,11... | collective-permute-start | bytes 589832 | tf_op jit(solution)/shard_map/ppermute | solution.py:482
  13.9 0.9 %copy-start = (f32[12,4,8,128]{3,2,1,0:T(8,128)S(1)}, f32[12,4,8,128]{3,2,1,0:T(8,128)}, u32[]{:S(2)}) copy-start(f32[12,4,8,128]{3,2,1,0:T(8,128)} %get-tuple-element.51.source) | copy-start | bytes 589828
  16.2 1.7 %copy-start.5 = (s32[3]{0:T(128)S(1)}, s32[3]{0:T(128)}, u32[]{:S(2)}) copy-start(s32[3]{0:T(128)} %refs_0_.3) | copy-start | bytes 40
  16.2 1.7 %copy-start.6 = (f32[9]{0:T(128)S(1)}, f32[9]{0:T(128)}, u32[]{:S(2)}) copy-start(f32[9]{0:T(128)} %refs_1_.3) | copy-start | bytes 112
  16.2 1.7 %copy-start.7 = (s32[3]{0:T(128)S(1)}, s32[3]{0:T(128)}, u32[]{:S(2)}) copy-start(s32[3]{0:T(128)} %refs_2_.3) | copy-start | bytes 40
  22.1 5.7 %collective-permute-start.13 = (f32[4,4,8,256]{3,2,1,0:T(8,128)S(1)}, f32[4,4,8,256]{3,2,1,0:T(8,128)S(1)}, u32[]{:S(2)}, u32[]{:S(2)}) collective-permute-start(f32[4,4,8,256]{3,2,1,0:T(8,128)S(1)} %get-tuple-element.55), channel_id=1, source_target_pairs={{0,2},{1,3},{2,0},{3,1},{4,6},{5,7},{6,4},{7,5},{8,10},{9,11},{10,... | collective-permute-start | bytes 393224 | tf_op jit(solution)/shard_map/ppermute | solution.py:482
  23.6 9.2 %collective-permute-start.16 = (f32[8,4,8,256]{3,2,1,0:T(8,128)S(1)}, f32[8,4,8,256]{3,2,1,0:T(8,128)S(1)}, u32[]{:S(2)}, u32[]{:S(2)}) collective-permute-start(f32[8,4,8,256]{3,2,1,0:T(8,128)S(1)} %get-tuple-element.54.refs_3_), channel_id=1, source_target_pairs={{0,16},{1,4},{2,18},{3,6},{4,1},{5,8},{6,3},{7,10},{8,5},{9,12},{1... | collective-permute-start | bytes 786440 | tf_op jit(solution)/shard_map/ppermute | solution.py:482
  25.1 7.7 %collective-permute-start.14 = (f32[8,4,8,256]{3,2,1,0:T(8,128)S(1)}, f32[8,4,8,256]{3,2,1,0:T(8,128)S(1)}, u32[]{:S(2)}, u32[]{:S(2)}) collective-permute-start(f32[8,4,8,256]{3,2,1,0:T(8,128)S(1)} %get-tuple-element.54.refs_3_), channel_id=1, source_target_pairs={{0,1},{1,0},{2,3},{3,2},{4,5},{5,4},{6,7},{7,6},{8,9},{9,8},{10,11... | collective-permute-start | bytes 786440 | tf_op jit(solution)/shard_map/ppermute | solution.py:482
  27.8 5.0 %collective-permute-start.17 = (f32[4,4,8,256]{3,2,1,0:T(8,128)S(1)}, f32[4,4,8,256]{3,2,1,0:T(8,128)S(1)}, u32[]{:S(2)}, u32[]{:S(2)}) collective-permute-start(f32[4,4,8,256]{3,2,1,0:T(8,128)S(1)} %collective-permute-done.13.refs_4_), channel_id=1, source_target_pairs={{0,16},{1,4},{2,18},{3,6},{4,1},{5,8},{6,3},{7,10},{8,5},{9,12},{1... | collective-permute-start | bytes 393224 | tf_op jit(solution)/shard_map/ppermute | solution.py:482
  29.0 3.8 %collective-permute-start.15 = (f32[4,4,8,256]{3,2,1,0:T(8,128)S(1)}, f32[4,4,8,256]{3,2,1,0:T(8,128)S(1)}, u32[]{:S(2)}, u32[]{:S(2)}) collective-permute-start(f32[4,4,8,256]{3,2,1,0:T(8,128)S(1)} %collective-permute-done.13.refs_4_), channel_id=1, source_target_pairs={{0,1},{1,0},{2,3},{3,2},{4,5},{5,4},{6,7},{7,6},{8,9},{9,8},{10,11... | collective-permute-start | bytes 393224 | tf_op jit(solution)/shard_map/ppermute | solution.py:482
  36.5 7.3 %copy-start.4 = (s32[48,2]{0,1:T(2,128)S(1)}, s32[48,2]{0,1:T(2,128)}, u32[]{:S(2)}) copy-start(s32[48,2]{0,1:T(2,128)} %param.25) | copy-start | bytes 1156
  36.5 1.4 %collective-permute-start.18 = (bf16[3,4,16,256]{3,2,1,0:T(8,128)(2,1)S(1)}, bf16[3,4,16,256]{3,2,1,0:T(8,128)(2,1)S(1)}, u32[]{:S(2)}, u32[]{:S(2)}) collective-permute-start(bf16[3,4,16,256]{3,2,1,0:T(8,128)(2,1)S(1)} %get-tuple-element.62.snaps), channel_id=1, source_target_pairs={{0,1},{1,0},{2,3},{3,2},{4,5},{5,4},{6,7},{7,6},{8,9},{9,8},{10,11... | collective-permute-start | bytes 294920 | tf_op jit(solution)/shard_map/ppermute | solution.py:482
  36.6 4.7 %collective-permute-start.19 = (bf16[3,4,16,256]{3,2,1,0:T(8,128)(2,1)S(1)}, bf16[3,4,16,256]{3,2,1,0:T(8,128)(2,1)S(1)}, u32[]{:S(2)}, u32[]{:S(2)}) collective-permute-start(bf16[3,4,16,256]{3,2,1,0:T(8,128)(2,1)S(1)} %get-tuple-element.62.snaps), channel_id=1, source_target_pairs={{0,16},{1,4},{2,18},{3,6},{4,1},{5,8},{6,3},{7,10},{8,5},{9,12},{1... | collective-permute-start | bytes 294920 | tf_op jit(solution)/shard_map/ppermute | solution.py:482
  37.9 4.6 %collective-permute-start.20 = (bf16[3,4,16,256]{3,2,1,0:T(8,128)(2,1)S(1)}, bf16[3,4,16,256]{3,2,1,0:T(8,128)(2,1)S(1)}, u32[]{:S(2)}, u32[]{:S(2)}) collective-permute-start(bf16[3,4,16,256]{3,2,1,0:T(8,128)(2,1)S(1)} %collective-permute-done.18.sib), channel_id=1, source_target_pairs={{0,16},{1,4},{2,18},{3,6},{4,1},{5,8},{6,3},{7,10},{8,5},{9,12},{1... | collective-permute-start | bytes 294920 | tf_op jit(solution)/shard_map/ppermute | solution.py:482
  39.1 3.4 %collective-permute-start.23 = (f32[8,4,8,128]{3,2,1,0:T(8,128)S(1)}, f32[8,4,8,128]{3,2,1,0:T(8,128)S(1)}, u32[]{:S(2)}, u32[]{:S(2)}) collective-permute-start(f32[8,4,8,128]{3,2,1,0:T(8,128)S(1)} %get-tuple-element.64), channel_id=1, source_target_pairs={{0,1},{1,0},{2,3},{3,2},{4,5},{5,4},{6,7},{7,6},{8,9},{9,8},{10,11... | collective-permute-start | bytes 393224 | tf_op jit(solution)/shard_map/ppermute | solution.py:482
  41.3 2.0 %collective-permute-start.21 = (bf16[3,4,16,256]{3,2,1,0:T(8,128)(2,1)S(1)}, bf16[3,4,16,256]{3,2,1,0:T(8,128)(2,1)S(1)}, u32[]{:S(2)}, u32[]{:S(2)}) collective-permute-start(bf16[3,4,16,256]{3,2,1,0:T(8,128)(2,1)S(1)} %collective-permute-done.19.near), channel_id=1, source_target_pairs={{0,1},{1,0},{2,3},{3,2},{4,5},{5,4},{6,7},{7,6},{8,9},{9,8},{10,11... | collective-permute-start | bytes 294920 | tf_op jit(solution)/shard_map/ppermute | solution.py:482
  42.5 1.3 %collective-permute-start.22 = (bf16[3,4,16,256]{3,2,1,0:T(8,128)(2,1)S(1)}, bf16[3,4,16,256]{3,2,1,0:T(8,128)(2,1)S(1)}, u32[]{:S(2)}, u32[]{:S(2)}) collective-permute-start(bf16[3,4,16,256]{3,2,1,0:T(8,128)(2,1)S(1)} %collective-permute-done.20.far), channel_id=1, source_target_pairs={{0,1},{1,0},{2,3},{3,2},{4,5},{5,4},{6,7},{7,6},{8,9},{9,8},{10,11... | collective-permute-start | bytes 294920 | tf_op jit(solution)/shard_map/ppermute | solution.py:482
  (3 other events, 2.3 us)
